TPU v7x, 512 devices: a whole 4x4x16 slice. The times are simulated.
512 devices in a mesh: dp: 16 (over x, y), expert: 32 (over z, core).
Axes of the slice: x: 4, y: 4, z: 16, core: 2. Of those that a mesh axis runs over, the one named last changes fastest.
Arguments:
- tokens: bfloat16 [1024, 4096], P('expert', 'dp'), may hold values from -6 to 6
- expert_ids: int32 [1024, 8], P('expert'), may hold values from 0 to 31, all different within a row; in each aligned block of 32 rows (0 to 31, 32 to 63, ...) at most 16 rows name the same one
- route_weights: float32 [1024, 8], P('expert'), may hold values from 0.1 to 1
- gate_weight: bfloat16 [32, 1536, 4096], P('expert', None, 'dp'), may hold values from -0.09375 to 0.09375
- up_weight: bfloat16 [32, 1536, 4096], P('expert', None, 'dp'), may hold values from -0.09375 to 0.09375
- down_weight: bfloat16 [32, 1536, 4096], P('expert', None, 'dp'), may hold values from -0.15625 to 0.15625
- output_grad: bfloat16 [1024, 4096], P('expert', 'dp'), may hold values from -1.5 to 1.5
Outputs:
- layer_output: bfloat16 [1024, 4096], P('expert', 'dp')
- token_gradient: bfloat16 [1024, 4096], P('expert', 'dp')
- route_gradient: float32 [1024, 8], P('expert')
- gate_gradient: bfloat16 [32, 1536, 4096], P('expert', None, 'dp')
- up_gradient: bfloat16 [32, 1536, 4096], P('expert', None, 'dp')
- down_gradient: bfloat16 [32, 1536, 4096], P('expert', None, 'dp')
Inputs may be any that keep to these rules, and one draw needn't show every extreme that they name: `expert_ids`: within each aligned block of 32 tokens no expert is named more than 16 times, and in every draw some block names some expert exactly 16 times; the experts of one token differ.
All inputs are finite; a program needn't handle non-finite values.
Results may differ from a plain program's by a relative error of at most 0.023.
Values may be sent and summed in bfloat16 or wider, within the bound.
A program may use at most 64 MiB of HBM per device.

v0:
```python
import jax
import jax.numpy as jnp
from jax import lax
from jax.sharding import PartitionSpec as P

highest = lax.Precision.HIGHEST


def build_slots(expert_ids, experts, capacity):
    tok_count, top_count = expert_ids.shape
    flat_ids = expert_ids.reshape(tok_count * top_count)
    member = (flat_ids[:, None] == jnp.arange(experts, dtype=jnp.int32)[None, :]).astype(jnp.int32)
    before = jnp.cumsum(member, axis=0) - member
    rank_in = jnp.sum(before * member, axis=1)
    slot_ids = flat_ids * capacity + rank_in
    table = slot_ids[:, None] == jnp.arange(experts * capacity, dtype=jnp.int32)[None, :]
    return table.reshape(tok_count, top_count, experts * capacity).astype(jnp.float32)


def to_experts(spread, row_block):
    placed = lax.dot_general(
        spread, row_block.astype(jnp.float32), (((0,), (0,)), ((), ())), precision=highest
    )
    return lax.all_to_all(
        placed.astype(jnp.bfloat16), "expert", split_axis=0, concat_axis=0, tiled=True
    )


def from_experts(rows_out):
    return lax.all_to_all(rows_out, "expert", split_axis=0, concat_axis=0, tiled=True).astype(
        jnp.float32
    )


def contract_first(lhs_matrix, rhs_matrix):
    return lax.dot_general(
        lhs_matrix, rhs_matrix, (((0,), (0,)), ((), ())), preferred_element_type=jnp.float32
    )


def contract_last(lhs_matrix, rhs_matrix):
    return lax.dot_general(
        lhs_matrix, rhs_matrix, (((1,), (1,)), ((), ())), preferred_element_type=jnp.float32
    )


def activate(gate_pre, up_pre):
    sigmoid_gate = jax.nn.sigmoid(gate_pre)
    silu_gate = gate_pre * sigmoid_gate
    return (silu_gate * up_pre).astype(jnp.bfloat16)


def deltas(hidden_grad, gate_pre, up_pre):
    sigmoid_gate = jax.nn.sigmoid(gate_pre)
    silu_gate = gate_pre * sigmoid_gate
    silu_slope = sigmoid_gate * (1.0 + gate_pre * (1.0 - sigmoid_gate))
    gate_delta = (hidden_grad * up_pre * silu_slope).astype(jnp.bfloat16)
    up_delta = (hidden_grad * silu_gate).astype(jnp.bfloat16)
    return (gate_delta, up_delta)


def local(tokens, expert_ids, route_weights, gate_weight, up_weight, down_weight, output_grad):
    experts = lax.axis_size("expert")
    tok_count, top_count = expert_ids.shape
    capacity = min(2 * tok_count * top_count // experts, tok_count)
    table = build_slots(expert_ids, experts, capacity)
    picked = jnp.sum(table, axis=1)
    weighted = jnp.sum(table * route_weights[:, :, None], axis=1)
    gate_matrix = gate_weight[0]
    up_matrix = up_weight[0]
    down_matrix = down_weight[0]
    arrived = to_experts(picked, tokens)
    gate_part = contract_last(arrived, gate_matrix)
    up_part = contract_last(arrived, up_matrix)
    gate_pre, up_pre = (
        lax.psum(gate_part.astype(jnp.bfloat16), "dp").astype(jnp.float32),
        lax.psum(up_part.astype(jnp.bfloat16), "dp").astype(jnp.float32),
    )
    hidden_act = activate(gate_pre, up_pre)
    expert_out = jnp.dot(hidden_act, down_matrix, preferred_element_type=jnp.float32).astype(
        jnp.bfloat16
    )
    returned = from_experts(expert_out)
    layer_output = jnp.dot(weighted, returned, precision=highest).astype(jnp.bfloat16)
    slot_grad = lax.dot_general(
        output_grad.astype(jnp.float32), returned, (((1,), (1,)), ((), ())), precision=highest
    )
    own_terms = jnp.sum(table * slot_grad[:, None, :], axis=2)
    route_gradient = lax.psum(own_terms, "dp")
    grad_rows = to_experts(weighted, output_grad)
    grad_part = contract_last(grad_rows, down_matrix)
    hidden_grad = lax.psum(grad_part.astype(jnp.bfloat16), "dp").astype(jnp.float32)
    gate_delta, up_delta = deltas(hidden_grad, gate_pre, up_pre)
    down_gradient = contract_first(hidden_act, grad_rows).astype(jnp.bfloat16)
    gate_gradient = contract_first(gate_delta, arrived).astype(jnp.bfloat16)
    up_gradient = contract_first(up_delta, arrived).astype(jnp.bfloat16)
    back_out = jnp.dot(gate_delta, gate_matrix, preferred_element_type=jnp.float32)
    back_out = back_out + jnp.dot(up_delta, up_matrix, preferred_element_type=jnp.float32)
    back_rows = from_experts(back_out.astype(jnp.bfloat16))
    token_gradient = jnp.dot(picked, back_rows, precision=highest).astype(jnp.bfloat16)
    return (
        layer_output,
        token_gradient,
        route_gradient,
        gate_gradient[None],
        up_gradient[None],
        down_gradient[None],
    )


def solution(mesh):
    placed = (
        P("expert", "dp"),
        P("expert", None),
        P("expert", None),
        P("expert", None, "dp"),
        P("expert", None, "dp"),
        P("expert", None, "dp"),
        P("expert", "dp"),
    )
    return jax.shard_map(
        local,
        mesh=mesh,
        in_specs=placed,
        out_specs=(
            P("expert", "dp"),
            P("expert", "dp"),
            P("expert", None),
            P("expert", None, "dp"),
            P("expert", None, "dp"),
            P("expert", None, "dp"),
        ),
        check_vma=False,
    )
```

profile of v0, /device:TPU:64, one launch (start us, length us, event | category | flops | bytes accessed | tf_op | source)
XLA Modules:
  0.0 455.6 jit_solution(9990499533742959057)
XLA Ops:
  7.2 0.0 copy-start
  7.2 0.0 copy-start.4
  7.2 0.0 all-reduce.6.cloned.1.call-start
  7.2 0.9 copy.20
  8.1 0.1 eq.43
  8.2 0.1 eq.39
  8.3 0.6 reduce-window.6
  8.9 0.2 slice_reduce_fusion
  9.1 0.1 fusion.22
  9.2 0.1 reduce_sum.39
  9.3 0.2 convert_reduce_fusion
  9.6 1.1 convolution_convert_fusion.7
  10.7 0.0 copy-start.3
  10.7 33.6 %all_to_all.48 = bf16[32,16,256]{2,1,0:T(8,128)(2,1)S(1)} all-to-all(bf16[32,16,256]{2,1,0:T(8,128)(2,1)S(1)} %bitcast.81), channel_id=1, replica_groups=mesh['dp'=16,'expert'=32] {'expert'}, dimensions={0} | all-to-all | bytes 524288 | tf_op jit(solution)/shard_map/all_to_all | solution.py:24
  44.3 0.0 copy-done.4
  44.3 1.8 convolution_convert_fusion.1
  46.1 0.0 copy-done.3
  46.1 1.8 convolution_convert_fusion.2
  47.9 0.0 all-reduce.6.cloned.1.call-update
  47.9 121.7 %all-reduce.6.cloned.1.call-done = (bf16[512,1536]{1,0:T(8,128)(2,1)}, bf16[512,1536]{1,0:T(8,128)(2,1)}) async-done(((bf16[512,1536]{1,0:T(8,128)(2,1)}, bf16[512,1536]{1,0:T(8,128)(2,1)}), (bf16[512,1536]{1,0:T(8,128)(2,1)}, bf16[512,1536]{1,0:T(8,128)(2,1)})) %all-reduce.6.cloned.1.call-update) | async-done | bytes 3145744 | tf_op jit(solution)/shard_map/psum | solution.py:77
  169.6 2.8 fusion
  172.5 0.0 copy-start.8
  172.5 1.1 copy-done.8
  173.6 0.0 copy-done
  173.6 0.0 copy-start.12
  173.6 0.0 copy-start.11
  173.6 1.3 convolution_convert_fusion.8
  174.9 12.7 %all-to-all-start.1 = ((bf16[32,16,256]{2,1,0:T(8,128)(2,1)}), bf16[32,16,256]{2,1,0:T(8,128)(2,1)S(1)}, u32[]{:S(2)}, u32[]{:S(2)}) async-start(bf16[32,16,256]{2,1,0:T(8,128)(2,1)} %bitcast.6), calls=%async_computation.1 | async-start | bytes 524288 | tf_op jit(solution)/shard_map/all_to_all | solution.py:30
  187.6 0.0 all-reduce.4.cloned.1.call-start
  187.7 0.0 copy-done.12
  187.7 0.1 copy.24
  187.8 18.6 %all-to-all-done.1 = bf16[32,16,256]{2,1,0:T(8,128)(2,1)S(1)} async-done(((bf16[32,16,256]{2,1,0:T(8,128)(2,1)}), bf16[32,16,256]{2,1,0:T(8,128)(2,1)S(1)}, u32[]{:S(2)}, u32[]{:S(2)}) %all-to-all-start.1) | async-done | bytes 262176 | tf_op jit(solution)/shard_map/all_to_all | solution.py:30
  206.4 0.0 copy-start.6
  206.4 0.0 copy-done.11
  206.4 0.2 convolution_bitcast_fusion
  206.6 0.9 select_reduce_fusion
  207.5 0.4 convolution_convert_fusion.6
  207.9 25.6 %all_to_all.49 = bf16[32,16,256]{2,1,0:T(8,128)(2,1)S(1)} all-to-all(bf16[32,16,256]{2,1,0:T(8,128)(2,1)S(1)} %bitcast.82), channel_id=1, replica_groups=mesh['dp'=16,'expert'=32] {'expert'}, dimensions={0} | all-to-all | bytes 524288 | tf_op jit(solution)/shard_map/all_to_all | solution.py:24
  233.5 0.0 copy-start.9
  233.5 0.7 copy-done.9
  234.2 1.8 convolution_convert_fusion
  236.0 0.0 copy-done.6
  236.0 0.0 all-reduce.4.cloned.1.call-update
  236.0 112.5 %all-reduce.4.cloned.1.call-done = bf16[512,1536]{1,0:T(8,128)(2,1)} async-done(((bf16[512,1536]{1,0:T(8,128)(2,1)}), bf16[512,1536]{1,0:T(8,128)(2,1)}) %all-reduce.4.cloned.1.call-update) | async-done | bytes 1572880 | tf_op jit(solution)/shard_map/psum | solution.py:92
  348.5 4.0 fusion.3
  352.5 0.0 copy-start.1
  352.6 0.0 copy-start.5
  352.6 0.6 fusion.17
  353.1 1.1 copy-done.5
  354.3 0.0 copy-start.7
  354.3 1.3 fusion.12
  355.6 0.0 copy-done.1
  355.6 12.7 %all-to-all-start.3 = ((bf16[32,16,256]{2,1,0:T(8,128)(2,1)}), bf16[32,16,256]{2,1,0:T(8,128)(2,1)S(1)}, u32[]{:S(2)}, u32[]{:S(2)}) async-start(bf16[32,16,256]{2,1,0:T(8,128)(2,1)} %bitcast.10), calls=%async_computation.3 | async-start | bytes 524288 | tf_op jit(solution)/shard_map/all_to_all | solution.py:30
  368.3 72.1 %psum.31 = f32[32,8]{1,0:T(8,128)S(1)} all-reduce(f32[32,8]{1,0:T(8,128)} %get-tuple-element.12), channel_id=1, replica_groups=mesh['dp'=16,'expert'=32] {'dp'}, use_global_device_ids=true, to_apply=%region_9.10 | all-reduce | flops 256 | bytes 2048 | tf_op jit(solution)/shard_map/psum | solution.py:89
  440.4 0.7 copy.25
  441.0 0.0 copy-done.7
  441.0 0.9 convolution_convert_fusion.10
  441.9 0.0 copy-done.10
  441.9 3.0 fusion.11
  444.9 0.0 copy-done.2
  444.9 1.5 fusion.9
  446.4 1.5 fusion.10
  447.9 0.0 all-to-all-done.3
  447.9 0.9 convolution_convert_fusion.9
  (6 shorter events, 0.1 us)
Async XLA Ops:
  7.2 166.5 %copy-start = (bf16[1,1536,256]{2,1,0:T(8,128)(2,1)S(1)}, bf16[1,1536,256]{2,1,0:T(8,128)(2,1)}, u32[]{:S(2)}) copy-start(bf16[1,1536,256]{2,1,0:T(8,128)(2,1)} %param.12) | copy-start | bytes 2359300
  7.2 37.2 %copy-start.4 = (bf16[1,1536,256]{2,1,0:T(8,128)(2,1)S(1)}, bf16[1,1536,256]{2,1,0:T(8,128)(2,1)}, u32[]{:S(2)}) copy-start(bf16[1,1536,256]{2,1,0:T(8,128)(2,1)} %param.11) | copy-start | bytes 2359300
  7.2 162.4 %all-reduce.6.cloned.1.call-start = ((), (), s32[]{:S(2)}) async-start(), calls=%async_computation.5 | async-start | bytes 6291456 | tf_op jit(solution)/shard_map/psum | solution.py:77
  10.7 35.4 %copy-start.3 = (bf16[1,1536,256]{2,1,0:T(8,128)(2,1)S(1)}, bf16[1,1536,256]{2,1,0:T(8,128)(2,1)}, u32[]{:S(2)}) copy-start(bf16[1,1536,256]{2,1,0:T(8,128)(2,1)} %param.10) | copy-start | bytes 2359300
  172.5 1.2 copy-start.8
  173.6 14.1 %copy-start.12 = (f32[32,8]{0,1:T(8,128)S(1)}, f32[32,8]{0,1:T(8,128)}, u32[]{:S(2)}) copy-start(f32[32,8]{0,1:T(8,128)} %param.9) | copy-start | bytes 3076
  173.6 32.8 %copy-start.11 = (bf16[32,256]{1,0:T(8,128)(2,1)S(1)}, bf16[32,256]{1,0:T(8,128)(2,1)}, u32[]{:S(2)}) copy-start(bf16[32,256]{1,0:T(8,128)(2,1)} %param.13) | copy-start | bytes 49156
  174.9 31.5 %all-to-all-start.1 = ((bf16[32,16,256]{2,1,0:T(8,128)(2,1)}), bf16[32,16,256]{2,1,0:T(8,128)(2,1)S(1)}, u32[]{:S(2)}, u32[]{:S(2)}) async-start(bf16[32,16,256]{2,1,0:T(8,128)(2,1)} %bitcast.6), calls=%async_computation.1 | async-start | bytes 524288 | tf_op jit(solution)/shard_map/all_to_all | solution.py:30
  187.6 160.9 %all-reduce.4.cloned.1.call-start = ((), (), s32[]{:S(2)}) async-start(), calls=%async_computation.4 | async-start | bytes 3145728 | tf_op jit(solution)/shard_map/psum | solution.py:92
  206.4 29.6 %copy-start.6 = (bf16[32,16,256]{2,1,0:T(8,128)(2,1)}, bf16[32,16,256]{2,1,0:T(8,128)(2,1)S(1)}, u32[]{:S(2)}) copy-start(bf16[32,16,256]{2,1,0:T(8,128)(2,1)S(1)} %all-to-all-done.1) | copy-start | bytes 786436
  233.5 0.7 copy-start.9
  352.5 3.0 copy-start.1
  352.6 1.7 copy-start.5
  354.3 86.8 %copy-start.7 = (bf16[32,16,256]{2,1,0:T(8,128)(2,1)S(1)}, bf16[32,16,256]{2,1,0:T(8,128)(2,1)}, u32[]{:S(2)}) copy-start(bf16[32,16,256]{2,1,0:T(8,128)(2,1)} %copy-done.6) | copy-start | bytes 786436
  354.3 87.6 %copy-start.10 = (bf16[32,16,256]{2,1,0:T(8,128)(2,1)S(1)}, bf16[32,16,256]{2,1,0:T(8,128)(2,1)}, u32[]{:S(2)}) copy-start(bf16[32,16,256]{2,1,0:T(8,128)(2,1)} %copy-done.9) | copy-start | bytes 786436
  355.6 92.4 %all-to-all-start.3 = ((bf16[32,16,256]{2,1,0:T(8,128)(2,1)}), bf16[32,16,256]{2,1,0:T(8,128)(2,1)S(1)}, u32[]{:S(2)}, u32[]{:S(2)}) async-start(bf16[32,16,256]{2,1,0:T(8,128)(2,1)} %bitcast.10), calls=%async_computation.3 | async-start | bytes 524288 | tf_op jit(solution)/shard_map/all_to_all | solution.py:30
  441.9 3.0 copy-start.2
Sparse Core Ops, SparseCore 0:
  48.0 121.5 all-reduce.5
  236.1 112.3 all-reduce.3
where the time goes:
time: 457 us; the launch traced here: 456 us
  waiting for transfers between devices  253 us (55%)
  blocking collectives  131 us (29%)
  starting transfers between devices  25.5 us (6%)
  matrix products  17.9 us (4%)
  between operations  14.2 us (3%)
  other arithmetic  8.76 us (2%)
  local copies, waits for them, and re-layouts  5.06 us (1%)
    psum x1, waiting for transfers between devices, local(): lax.psum(up_part.astype(jnp.bfloat16), 'dp').astype(jnp.float32)  122 us
    psum x1, waiting for transfers between devices, local(): lax.psum(grad_part.astype(jnp.bfloat16), 'dp').astype(jnp.float32)  113 us
    psum x1, blocking collectives, local(): route_gradient = lax.psum(own_terms, 'dp')  72.1 us
    all_to_all x2, blocking collectives, to_experts(): lax.all_to_all(placed.astype(jnp.bfloat16), 'expert', split_axis=0, conca...  59.2 us
    all_to_all x2, starting transfers between devices, from_experts(): lax.all_to_all(rows_out, 'expert', split_axis=0, concat_axis=0, tiled=True)  25.4 us
    all_to_all x2, waiting for transfers between devices, from_experts(): lax.all_to_all(rows_out, 'expert', split_axis=0, concat_axis=0, tiled=True)  18.6 us
  transfers between devices with their start and end apart: 4, of which 3 were waited for; matrix products, arithmetic and copies ran while one was open for 2% of the time, Pallas kernels for 0%

commit v1 on v0

v1 whole, which is shorter than its diff:
```python
import jax
import jax.numpy as jnp
from jax import lax
from jax.experimental import pallas as pl
from jax.experimental.pallas import tpu as pltpu
from jax.sharding import PartitionSpec as P

MESH = pl.DeviceIdType.MESH
BF = jnp.bfloat16
F32 = jnp.float32

WAVES = ((0, 15, 1, 14), (2, 13, 3, 12), (4, 11, 5, 10), (6, 9, 7, 8))
NZ = 16
NW = 4
LAG = 2
STAGES = 9


def dot_last(a, b):
    return lax.dot_general(a, b, (((1,), (1,)), ((), ())), preferred_element_type=F32)


def dot_first(a, b):
    return lax.dot_general(a, b, (((0,), (0,)), ((), ())), preferred_element_type=F32)


def dot_plain(a, b):
    return lax.dot_general(a, b, (((1,), (0,)), ((), ())), preferred_element_type=F32)


def kernel(
    tok, ids, rw, og, wg, wu, wd,
    lo_out, tg_out, rg_out, gg, ug, dg,
    W, G, X, GD, WC, S, M1P, M1M, RP, RM, Q1P, Q1M, QP, QM, A, H3, RET, RR, OUT,
    w_sem, o_sem, z_snd, z_rcv, b_snd, b_rcv, s_snd, s_rcv, a_snd, a_rcv, t_snd, t_rcv,
):
    dp = lax.axis_index("dp")
    e = lax.axis_index("expert")
    x, y = dp // 4, dp % 4
    z, c = e // 2, e % 2
    pos = (x, y)

    def along(axis, step):
        if axis == 0:
            return {"dp": lax.rem(x + step, 4) * 4 + y}
        return {"dp": x * 4 + lax.rem(y + step, 4)}

    def on_z(step, other):
        return {"expert": lax.rem(z + step, NZ) * 2 + ((1 - c) if other else c)}

    loads = [
        pltpu.make_async_copy(src, W.at[n], w_sem.at[n]) for n, src in enumerate((wg, wu, wd))
    ]
    for load in loads:
        load.start()

    barrier = pltpu.get_barrier_semaphore()
    for axis in (0, 1):
        for step in (1, 3):
            pl.semaphore_signal(barrier, inc=1, device_id=along(axis, step), device_id_type=MESH)

    def greet(d, carry):
        pl.semaphore_signal(
            barrier, inc=1, device_id={"expert": lax.rem(e + d, 2 * NZ)}, device_id_type=MESH
        )
        return carry

    lax.fori_loop(1, 2 * NZ, greet, 0)

    lane = lax.broadcasted_iota(jnp.int32, (32, 128), 1)
    ex = lane % 32
    dense = jnp.zeros((32, 128), F32)
    member = jnp.zeros((32, 128), F32)
    for k in range(8):
        hit = ex == ids[:, k : k + 1]
        dense = dense + jnp.where(hit, rw[:, k : k + 1], 0.0)
        member = member + jnp.where(hit, 1.0, 0.0)
    tri = lax.broadcasted_iota(jnp.int32, (32, 32), 1) < lax.broadcasted_iota(jnp.int32, (32, 32), 0)
    before = dot_plain(jnp.where(tri, 1.0, 0.0).astype(BF), member.astype(BF))
    code = member * (before + 1.0)
    hi = dense.astype(BF)
    rest = dense - hi.astype(F32)
    mid = rest.astype(BF)
    low = (rest - mid.astype(F32)).astype(BF)
    meta = jnp.where(
        lane < 32,
        code,
        jnp.where(lane < 64, hi.astype(F32), jnp.where(lane < 96, mid.astype(F32), low.astype(F32))),
    )
    G[0, 0, :, 0:256] = tok[...]
    G[0, 0, :, 256:512] = og[...]
    G[0, 0, :, 512:640] = meta.astype(BF)

    pl.semaphore_wait(barrier, 2 * NZ - 1 + 4)

    sent = []

    def send(src, dst, snd, rcv, to):
        copy = pltpu.make_async_remote_copy(
            src_ref=src, dst_ref=dst, send_sem=snd, recv_sem=rcv, device_id=to, device_id_type=MESH
        )
        copy.start()
        sent.append(copy)
        return copy

    ring = {}

    def ring_send(s):
        ring[0, s] = send(
            G.at[0, (1 - s) % NZ], G.at[0, (-s) % NZ], z_snd.at[0, s], z_rcv.at[0, s], on_z(1, False)
        )
        if s < 8:
            ring[1, s] = send(
                G.at[0, s - 1], G.at[0, s], z_snd.at[1, s], z_rcv.at[1, s], on_z(NZ - 1, False)
            )

    def sib_send(r):
        ring["s", r] = send(G.at[0, r], G.at[1, r], b_snd.at[r], b_rcv.at[r], on_z(0, True))

    pumped = [0]

    def pump(upto):
        while pumped[0] < min(upto, 8):
            pumped[0] += 1
            s = pumped[0]
            ring[0, s].wait_recv()
            if s < 8:
                ring[1, s].wait_recv()
                ring_send(s + 1)
            sib_send((-s) % NZ)
            if s < 8:
                sib_send(s)

    ring_send(1)
    sib_send(0)

    made = {}

    def ring_pair(key, fwd, back, axis):
        for n, (src, dst) in enumerate(fwd):
            made[key, 0, n] = send(src, dst, *sems(key, 0, n), along(axis, 1))
        for n, (src, dst) in enumerate(back):
            made[key, 1, n] = send(src, dst, *sems(key, 1, n), along(axis, 3))

    def sems(key, d, n):
        kind, w, h, ph = key
        if kind == "s":
            return s_snd.at[w, h, ph, d, n], s_rcv.at[w, h, ph, d, n]
        return a_snd.at[w, h, ph, d, n], a_rcv.at[w, h, ph, d, n]

    def arrived(key, d, n):
        made[key, d, n].wait_recv()

    def reduce_start(w, h, ph):
        axis = h if ph == 0 else 1 - h
        i = pos[axis]
        if ph == 0:
            part = lambda t, us: S.at[w, h, t, :, us]
            m1p, m1m, rp, rm = M1P.at[w, h], M1M.at[w, h], RP, RM
            into = lambda r, us: r.at[w, h, :, us]
        else:
            own = pos[h]
            part = lambda t, us: S.at[w, h, own, t, us]
            m1p, m1m, rp, rm = Q1P.at[w, h], Q1M.at[w, h], QP, QM
            into = lambda r, us: r.at[w, h, us]
        L, R = pl.ds(0, 5), pl.ds(5, 4)
        two, nxt, prv = lax.rem(i + 2, 4), lax.rem(i + 1, 4), lax.rem(i + 3, 4)
        ring_pair(
            ("s", w, h, ph),
            ((part(two, L), m1p), (part(nxt, R), into(rp, R))),
            ((part(two, R), m1m), (part(prv, L), into(rm, L))),
            axis,
        )

    def reduce_merge(w, h, ph):
        axis = h if ph == 0 else 1 - h
        i = pos[axis]
        key = ("s", w, h, ph)
        nxt, prv = lax.rem(i + 1, 4), lax.rem(i + 3, 4)
        L, R = pl.ds(0, 5), pl.ds(5, 4)
        if ph == 0:
            part = lambda t, us: S.at[w, h, t, :, us]
            m1p, m1m, rp, rm = M1P.at[w, h], M1M.at[w, h], RP, RM
            into = lambda r, us: r.at[w, h, :, us]
        else:
            own = pos[h]
            part = lambda t, us: S.at[w, h, own, t, us]
            m1p, m1m, rp, rm = Q1P.at[w, h], Q1M.at[w, h], QP, QM
            into = lambda r, us: r.at[w, h, us]
        for d, tgt, us, m1, r in ((0, nxt, L, m1p, rp), (1, prv, R, m1m, rm)):
            arrived(key, d, 0)
            ref = part(tgt, us)
            ref[...] = (ref[...].astype(F32) + m1[...].astype(F32)).astype(BF)
            made[key, d, 2] = send(ref, into(r, us), *sems(key, d, 2), along(axis, 1 if d == 0 else 3))

    def reduce_end(w, h, ph):
        key = ("s", w, h, ph)
        for d in (0, 1):
            arrived(key, d, 1)
            arrived(key, d, 2)
        if ph == 0:
            i = pos[h]
            total = S[w, h, i].astype(F32) + RP[w, h].astype(F32) + RM[w, h].astype(F32)
            S[w, h, i] = total.astype(BF)
            return None
        return S[w, h, pos[h], pos[1 - h]].astype(F32) + QP[w, h].astype(F32) + QM[w, h].astype(F32)

    def gather_start(w, h, ph):
        axis = 1 - h if ph == 0 else h
        i, j = pos[h], pos[1 - h]
        L, R = pl.ds(0, 5), pl.ds(5, 5 - h)
        part = (lambda us: A.at[w, h, i, j, us]) if ph == 0 else (lambda us: A.at[w, h, i, :, us])
        ring_pair(
            ("a", w, h, ph),
            ((part(L), part(L)), (part(R), part(R))),
            ((part(R), part(R)), (part(L), part(L))),
            axis,
        )

    def gather_forward(w, h, ph):
        axis = 1 - h if ph == 0 else h
        key = ("a", w, h, ph)
        i, j = pos[h], pos[1 - h]
        nxt, prv = lax.rem(pos[axis] + 1, 4), lax.rem(pos[axis] + 3, 4)
        L, R = pl.ds(0, 5), pl.ds(5, 5 - h)
        for d, src, us in ((0, prv, L), (1, nxt, R)):
            arrived(key, d, 0)
            ref = A.at[w, h, i, src, us] if ph == 0 else A.at[w, h, src, :, us]
            made[key, d, 2] = send(ref, ref, *sems(key, d, 2), along(axis, 1 if d == 0 else 3))

    def gather_end(w, h, ph):
        for d in (0, 1):
            arrived(("a", w, h, ph), d, 1)
            arrived(("a", w, h, ph), d, 2)

    def partials(w):
        blocks = [(r, o) for r in WAVES[w] for o in (0, 1)]
        pump(max(min(r, NZ - r) for r in WAVES[w]))
        for r in WAVES[w]:
            ring["s", r].wait_recv()
        tokens = jnp.concatenate([G[o, r, :, 0:256] for r, o in blocks], axis=0)
        grads = jnp.concatenate([G[o, r, :, 256:512] for r, o in blocks], axis=0)
        info_in = jnp.concatenate([G[o, r, :, 512:640] for r, o in blocks], axis=0)
        row = lax.broadcasted_iota(jnp.int32, (16, 128), 0)
        col = lax.broadcasted_iota(jnp.int32, (16, 128), 1)
        pick = jnp.where((col == row * 32 + e) & (row < 4), 1.0, 0.0).astype(BF)
        info = dot_last(pick, info_in)
        w_row = info[1:2] + info[2:3] + info[3:4]
        s_i = lax.broadcasted_iota(jnp.int32, (128, 256), 0)
        t_i = lax.broadcasted_iota(jnp.int32, (128, 256), 1)
        sel = (s_i // 16 == t_i // 32) & (info[0:1] == (s_i % 16 + 1).astype(F32))
        sel_b = jnp.where(sel, 1.0, 0.0).astype(BF)
        w_col = jnp.sum(jnp.where(sel, w_row, 0.0), axis=1, keepdims=True)
        rows = dot_plain(sel_b, tokens).astype(BF)
        rows_g = (dot_plain(sel_b, grads) * w_col).astype(BF)
        X[w] = rows
        GD[w] = rows_g
        WC[w] = jnp.broadcast_to(w_col, (128, 128)).reshape(8, 16, 128)
        for t in range(3):
            if w == 0:
                loads[t].wait()
            src = rows if t < 2 else rows_g
            for n in range(6):
                out = dot_last(src, W[t, n * 256 : (n + 1) * 256, :]).astype(BF)
                q = n // 3
                for part in (0, 1):
                    k = (n % 3) * 2 + part
                    h, u = k // 3, (k % 3) * 3 + t
                    for j in range(8):
                        tile = out[16 * j : 16 * j + 16, part * 128 : part * 128 + 128]
                        if h == 0:
                            S[w, 0, j // 2, 2 * (j % 2) + q, u] = tile
                        else:
                            S[w, 1, 2 * (j % 2) + q, j // 2, u] = tile
        for h in (0, 1):
            reduce_start(w, h, 0)

    def nonlinear(w):
        rg = jnp.zeros((16, 1), F32)
        for h in (0, 1):
            total = reduce_end(w, h, 1)
            i, j = pos[h], pos[1 - h]
            for k in range(3):
                gate, up, hid = total[3 * k], total[3 * k + 1], total[3 * k + 2]
                sig = jax.nn.sigmoid(gate)
                silu = gate * sig
                act = (silu * up).astype(BF)
                A[w, h, i, j, 3 * k] = act
                A[w, h, i, j, 3 * k + 1] = (hid * up * (sig * (1.0 + gate * (1.0 - sig)))).astype(BF)
                A[w, h, i, j, 3 * k + 2] = (hid * silu).astype(BF)
                rg = rg + jnp.sum(act.astype(F32) * hid, axis=1, keepdims=True)
        wc = WC[w, 2 * x + y // 2]
        used = wc > 0.0
        rg = jnp.where(used, rg / jnp.where(used, wc, 1.0), 0.0)
        A[w, 0, x, y, 9] = in_two(rg)
        for h in (0, 1):
            gather_start(w, h, 0)

    lane16 = lax.broadcasted_iota(jnp.int32, (16, 128), 1)

    def in_two(v):
        top = v.astype(BF).astype(F32)
        return jnp.where(lane16 < 64, top, v - top).astype(BF)

    back = {}

    def results(w):
        for h in (0, 1):
            gather_end(w, h, 1)
        base = w * 128
        for j in range(8):
            for q in (0, 1):
                for h in (0, 1):
                    for k in range(3):
                        for t in range(3):
                            if h == 0:
                                tile = A[w, 0, j // 2, 2 * (j % 2) + q, 3 * k + t]
                            else:
                                tile = A[w, 1, 2 * (j % 2) + q, j // 2, 3 * k + t]
                            at = q * 768 + (h * 3 + k) * 128
                            H3[t, base + 16 * j : base + 16 * j + 16, at : at + 128] = tile
        eo = dot_plain(H3[0, base : base + 128, :], W[2]).astype(BF)
        bo = dot_plain(H3[1, base : base + 128, :], W[0])
        bo = (bo + dot_plain(H3[2, base : base + 128, :], W[1])).astype(BF)
        for j in range(8):
            r, o = WAVES[w][j // 2], j % 2
            v = A[w, 0, j // 2, 2 * o, 9].astype(F32) + A[w, 0, j // 2, 2 * o + 1, 9].astype(F32)
            v = in_two(v + pltpu.roll(v, 64, 1))
            local = r == 0 and o == 0
            to = RR.at[0, 0] if local else RET.at[w, j]
            to[:, 0:256] = eo[16 * j : 16 * j + 16]
            to[:, 256:512] = bo[16 * j : 16 * j + 16]
            to[:, 512:640] = v
            if not local:
                m = (NZ - r) % NZ
                back[o, m] = send(
                    RET.at[w, j], RR.at[o, m], t_snd.at[o, m], t_rcv.at[o, m], on_z(r, o == 1)
                )

    def stage(k, w):
        if k == 0:
            partials(w)
        elif k == 4:
            nonlinear(w)
        elif k == 8:
            results(w)
        else:
            for h in (0, 1):
                if k == 1:
                    reduce_merge(w, h, 0)
                elif k == 2:
                    reduce_end(w, h, 0)
                    reduce_start(w, h, 1)
                elif k == 3:
                    reduce_merge(w, h, 1)
                elif k == 5:
                    gather_forward(w, h, 0)
                elif k == 6:
                    gather_end(w, h, 0)
                    gather_start(w, h, 1)
                elif k == 7:
                    gather_forward(w, h, 1)

    for tick in range(STAGES + LAG * (NW - 1)):
        pump(2 + 2 * tick)
        for w in range(NW):
            k = tick - LAG * w
            if 0 <= k < STAGES:
                stage(k, w)

    rows_x = X[...].reshape(512, 256)
    rows_g = GD[...].reshape(512, 256)
    stores = []
    for t, (n_h, rhs, dst) in enumerate(((1, rows_x, gg), (2, rows_x, ug), (0, rows_g, dg))):
        for n in range(6):
            cols = H3[n_h, :, n * 256 : (n + 1) * 256]
            OUT[t, n * 256 : (n + 1) * 256, :] = dot_first(cols, rhs).astype(BF)
        store = pltpu.make_async_copy(OUT.at[t], dst, o_sem.at[t])
        store.start()
        stores.append(store)

    s_i = lax.broadcasted_iota(jnp.int32, (128, 512), 1)
    l_i = lax.broadcasted_iota(jnp.int32, (128, 512), 0)

    def expert_of(s):
        blk = s // 16
        core = jnp.where(blk < NZ, c, 1 - c)
        return (z + blk % NZ) % NZ * 2 + core

    e_s = expert_of(s_i)
    pick_code = jnp.where(l_i == e_s, 1.0, 0.0).astype(BF)
    pick_w = jnp.where((l_i >= 32) & (l_i % 32 == e_s), 1.0, 0.0).astype(BF)
    own = G[0, 0, :, 512:640]
    code_s = dot_plain(own, pick_code)
    w_s = dot_plain(own, pick_w)
    s32 = lax.broadcasted_iota(jnp.int32, (32, 512), 1)
    chosen = code_s == (s32 % 16 + 1).astype(F32)
    weights = jnp.where(chosen, w_s, 0.0)
    w_hi = weights.astype(BF)
    w_lo = (weights - w_hi.astype(F32)).astype(BF)
    e32 = expert_of(s32)
    by_k = jnp.concatenate(
        [jnp.where(chosen & (e32 == ids[:, k : k + 1]), 1.0, 0.0) for k in range(8)], axis=0
    ).astype(BF)
    for copy in back.values():
        copy.wait_recv()
    back_eo = RR[:, :, :, 0:256].reshape(512, 256)
    back_bo = RR[:, :, :, 256:512].reshape(512, 256)
    back_rg = RR[:, :, :, 512:640].reshape(512, 128)
    lo_out[...] = (dot_plain(w_hi, back_eo) + dot_plain(w_lo, back_eo)).astype(BF)
    tg_out[...] = dot_plain(jnp.where(chosen, 1.0, 0.0).astype(BF), back_bo).astype(BF)
    both = dot_plain(by_k, back_rg)
    both = both + pltpu.roll(both, 64, 1)
    k_i = lax.broadcasted_iota(jnp.int32, (32, 8), 1)
    grad = jnp.zeros((32, 8), F32)
    for k in range(8):
        grad = grad + jnp.where(k_i == k, both[32 * k : 32 * k + 32, 0:1], 0.0)
    rg_out[...] = grad

    for store in stores:
        store.wait()
    for copy in sent:
        copy.wait_send()


def local(tokens, expert_ids, route_weights, gate_weight, up_weight, down_weight, output_grad):
    vmem = pl.BlockSpec(memory_space=pltpu.VMEM)
    hbm = pl.BlockSpec(memory_space=pl.ANY)
    wshape = jax.ShapeDtypeStruct((1536, 256), BF)
    dma = pltpu.SemaphoreType.DMA
    lo, tg, rg, gg, ug, dg = pl.pallas_call(
        kernel,
        out_shape=(
            jax.ShapeDtypeStruct((32, 256), BF),
            jax.ShapeDtypeStruct((32, 256), BF),
            jax.ShapeDtypeStruct((32, 8), F32),
            wshape,
            wshape,
            wshape,
        ),
        in_specs=[vmem, vmem, vmem, vmem, hbm, hbm, hbm],
        out_specs=[vmem, vmem, vmem, hbm, hbm, hbm],
        scratch_shapes=[
            pltpu.VMEM((3, 1536, 256), BF),
            pltpu.VMEM((2, NZ, 32, 640), BF),
            pltpu.VMEM((NW, 128, 256), BF),
            pltpu.VMEM((NW, 128, 256), BF),
            pltpu.VMEM((NW, 8, 16, 128), F32),
            pltpu.VMEM((NW, 2, 4, 4, 9, 16, 128), BF),
            pltpu.VMEM((NW, 2, 4, 5, 16, 128), BF),
            pltpu.VMEM((NW, 2, 4, 4, 16, 128), BF),
            pltpu.VMEM((NW, 2, 4, 9, 16, 128), BF),
            pltpu.VMEM((NW, 2, 4, 9, 16, 128), BF),
            pltpu.VMEM((NW, 2, 5, 16, 128), BF),
            pltpu.VMEM((NW, 2, 4, 16, 128), BF),
            pltpu.VMEM((NW, 2, 9, 16, 128), BF),
            pltpu.VMEM((NW, 2, 9, 16, 128), BF),
            pltpu.VMEM((NW, 2, 4, 4, 10, 16, 128), BF),
            pltpu.VMEM((3, 512, 1536), BF),
            pltpu.VMEM((NW, 8, 16, 640), BF),
            pltpu.VMEM((2, NZ, 16, 640), BF),
            pltpu.VMEM((3, 1536, 256), BF),
            dma((3,)),
            dma((3,)),
            dma((2, 9)),
            dma((2, 9)),
            dma((NZ,)),
            dma((NZ,)),
            dma((NW, 2, 2, 2, 3)),
            dma((NW, 2, 2, 2, 3)),
            dma((NW, 2, 2, 2, 3)),
            dma((NW, 2, 2, 2, 3)),
            dma((2, NZ)),
            dma((2, NZ)),
        ],
        compiler_params=pltpu.CompilerParams(
            collective_id=0, has_side_effects=True, vmem_limit_bytes=60 * 1024 * 1024
        ),
    )(
        tokens, expert_ids, route_weights, output_grad,
        gate_weight[0], up_weight[0], down_weight[0],
    )
    return lo, tg, rg, gg[None], ug[None], dg[None]


def solution(mesh):
    placed = (
        P("expert", "dp"),
        P("expert", None),
        P("expert", None),
        P("expert", None, "dp"),
        P("expert", None, "dp"),
        P("expert", None, "dp"),
        P("expert", "dp"),
    )
    return jax.shard_map(
        local,
        mesh=mesh,
        in_specs=placed,
        out_specs=(
            P("expert", "dp"),
            P("expert", "dp"),
            P("expert", None),
            P("expert", None, "dp"),
            P("expert", None, "dp"),
            P("expert", None, "dp"),
        ),
        check_vma=False,
    )
```

time: 457 us -> 132 us (0.29)
  the two profiles are of different devices: /device:TPU:64 before, /device:TPU:1 now
where the time goes in v1:
time: 132 us
  Pallas kernels  122 us (92%)
  local copies, waits for them, and re-layouts  9.17 us (7%)
    pallas_call x1, Pallas kernels, local(): pl.pallas_call(kernel, out_shape=(jax.ShapeDtypeStruct((32, 256), BF), ja...  122 us
    unnamed x22, local copies, waits for them, and re-layouts  9.17 us

profile of v1, /device:TPU:1, one launch (start us, length us, event | category | flops | bytes accessed | tf_op | source)
XLA Modules:
  0.0 131.7 jit_solution(12653306069155156714)
XLA Ops:
  0.6 0.0 copy-start.5
  0.6 0.7 copy-done.5
  1.3 0.0 copy-start.6
  1.3 0.7 copy.13.ids
  2.0 0.0 copy-done.6
  2.0 0.7 copy.14.rw
  2.7 121.9 %shard_map.118 = (bf16[32,256]{1,0:T(8,128)(2,1)}, bf16[32,256]{1,0:T(8,128)(2,1)}, f32[32,8]{1,0:T(8,128)}, bf16[1536,256]{1,0:T(8,128)(2,1)}, bf16[1536,256]{1,0:T(8,128)(2,1)}, /*index=5*/bf16[1536,256]{1,0:T(8,128)(2,1)}) custom-call(bf16[32,256]{1,0:T(8,128)(2,1)} %tok.1, s32[32,8]{1,0:T(8,128)} %copy.13.ids, f32[32,8]{1,0:T(8,128)} %copy.14.rw, ...), custom_call_target="tpu_custom_call" | custom-call | tf_op jit(solution)/shard_map/pallas_call | solution.py:431
  124.6 0.0 copy-start.2
  124.6 0.0 copy-start.4
  124.6 0.7 copy-done.2
  125.3 0.7 copy.15
  126.0 0.0 copy-done.4
  126.0 0.0 copy-start.3
  126.0 0.6 copy.21
  126.6 0.1 copy-done.3
  126.7 0.6 copy.22
  127.3 0.0 copy-start.1
  127.3 2.1 %copy.23 = bf16[1,1536,256]{2,1,0:T(8,128)(2,1)} copy(bf16[1,1536,256]{2,1,0:T(8,128)(2,1)} %bitcast.8) | data formatting | bytes 1572864
  129.4 0.0 copy-done.1
  129.4 0.0 copy-start
  129.4 0.9 copy.24
  130.3 0.5 copy-done
  130.9 0.9 copy.25
Async XLA Ops:
  0.6 0.7 copy-start.5
  1.3 0.7 copy-start.6
  124.6 0.7 copy-start.2
  124.6 1.4 %copy-start.4 = (bf16[32,256]{1,0:T(8,128)(2,1)S(1)}, bf16[32,256]{1,0:T(8,128)(2,1)}, u32[]{:S(2)}) copy-start(bf16[32,256]{1,0:T(8,128)(2,1)} %get-tuple-element.30) | copy-start | bytes 49156
  126.0 0.7 copy-start.3
  127.3 2.1 %copy-start.1 = (bf16[1536,256]{1,0:T(8,128)(2,1)S(1)}, bf16[1536,256]{1,0:T(8,128)(2,1)}, u32[]{:S(2)}) copy-start(bf16[1536,256]{1,0:T(8,128)(2,1)} %get-tuple-element.16) | copy-start | bytes 2359300
  129.4 1.4 %copy-start = (bf16[1536,256]{1,0:T(8,128)(2,1)S(1)}, bf16[1536,256]{1,0:T(8,128)(2,1)}, u32[]{:S(2)}) copy-start(bf16[1536,256]{1,0:T(8,128)(2,1)} %get-tuple-element.17) | copy-start | bytes 2359300

commit v2 on v1

--- a/solution.py
+++ b/solution.py
@@ -12,7 +12,7 @@
 WAVES = ((0, 15, 1, 14), (2, 13, 3, 12), (4, 11, 5, 10), (6, 9, 7, 8))
 NZ = 16
 NW = 4
-LAG = 2
+LAG = 1
 STAGES = 9
 
 
@@ -30,9 +30,9 @@
 
 def kernel(
     tok, ids, rw, og, wg, wu, wd,
-    lo_out, tg_out, rg_out, gg, ug, dg,
+    lo_out, tg_out, rg_out, grads_out,
     W, G, X, GD, WC, S, M1P, M1M, RP, RM, Q1P, Q1M, QP, QM, A, H3, RET, RR, OUT,
-    w_sem, o_sem, z_snd, z_rcv, b_snd, b_rcv, s_snd, s_rcv, a_snd, a_rcv, t_snd, t_rcv,
+    w_sem, o_sem, n_snd, n_rcv, z_snd, z_rcv, b_snd, b_rcv, s_snd, s_rcv, a_snd, a_rcv, t_snd, t_rcv,
 ):
     dp = lax.axis_index("dp")
     e = lax.axis_index("expert")
@@ -54,44 +54,45 @@
     for load in loads:
         load.start()
 
+    near = [along(axis, step) for axis in (0, 1) for step in (1, 3)]
+    near += [on_z(step, False) for step in (1, 2, NZ - 1, NZ - 2)] + [on_z(0, True)]
     barrier = pltpu.get_barrier_semaphore()
-    for axis in (0, 1):
-        for step in (1, 3):
-            pl.semaphore_signal(barrier, inc=1, device_id=along(axis, step), device_id_type=MESH)
-
-    def greet(d, carry):
-        pl.semaphore_signal(
-            barrier, inc=1, device_id={"expert": lax.rem(e + d, 2 * NZ)}, device_id_type=MESH
-        )
-        return carry
-
-    lax.fori_loop(1, 2 * NZ, greet, 0)
-
-    lane = lax.broadcasted_iota(jnp.int32, (32, 128), 1)
-    ex = lane % 32
-    dense = jnp.zeros((32, 128), F32)
-    member = jnp.zeros((32, 128), F32)
+    for peer in near:
+        pl.semaphore_signal(barrier, inc=1, device_id=peer, device_id_type=MESH)
+
+    sub = lax.broadcasted_iota(jnp.int32, (128, 32), 0)
+    ex = sub % 32
+    dense = jnp.zeros((128, 32), F32)
+    member = jnp.zeros((128, 32), F32)
+    ids_f = jnp.zeros((128, 32), F32)
     for k in range(8):
-        hit = ex == ids[:, k : k + 1]
-        dense = dense + jnp.where(hit, rw[:, k : k + 1], 0.0)
+        named = ids[k : k + 1, :]
+        hit = ex == named
+        dense = dense + jnp.where(hit, rw[k : k + 1, :], 0.0)
         member = member + jnp.where(hit, 1.0, 0.0)
-    tri = lax.broadcasted_iota(jnp.int32, (32, 32), 1) < lax.broadcasted_iota(jnp.int32, (32, 32), 0)
-    before = dot_plain(jnp.where(tri, 1.0, 0.0).astype(BF), member.astype(BF))
+        ids_f = ids_f + jnp.where(sub == k, named.astype(F32), 0.0)
+    tri = lax.broadcasted_iota(jnp.int32, (32, 32), 0) < lax.broadcasted_iota(jnp.int32, (32, 32), 1)
+    before = dot_plain(member.astype(BF), jnp.where(tri, 1.0, 0.0).astype(BF))
     code = member * (before + 1.0)
     hi = dense.astype(BF)
     rest = dense - hi.astype(F32)
     mid = rest.astype(BF)
     low = (rest - mid.astype(F32)).astype(BF)
     meta = jnp.where(
-        lane < 32,
+        sub < 32,
         code,
-        jnp.where(lane < 64, hi.astype(F32), jnp.where(lane < 96, mid.astype(F32), low.astype(F32))),
+        jnp.where(sub < 64, hi.astype(F32), jnp.where(sub < 96, mid.astype(F32), low.astype(F32))),
     )
+    eye = lax.broadcasted_iota(jnp.int32, (128, 128), 0) == lax.broadcasted_iota(
+        jnp.int32, (128, 128), 1
+    )
+    eye = jnp.where(eye, 1.0, 0.0).astype(BF)
     G[0, 0, :, 0:256] = tok[...]
     G[0, 0, :, 256:512] = og[...]
-    G[0, 0, :, 512:640] = meta.astype(BF)
-
-    pl.semaphore_wait(barrier, 2 * NZ - 1 + 4)
+    G[0, 0, :, 512:640] = dot_first(meta.astype(BF), eye).astype(BF)
+    ids_c = dot_first(ids_f.astype(BF), eye)
+
+    pl.semaphore_wait(barrier, len(near))
 
     sent = []
 
@@ -103,36 +104,52 @@
         sent.append(copy)
         return copy
 
+    first = []
+    for n, step in enumerate((1, NZ - 1, 2, NZ - 2)):
+        first.append(
+            send(G.at[0, 0], G.at[0, NZ - step], n_snd.at[n], n_rcv.at[n], on_z(step, False))
+        )
+    sib = {}
+
+    def sib_send(key, at, count):
+        n = len(sib)
+        sib[key] = send(
+            G.at[0, pl.ds(at, count)], G.at[1, pl.ds(at, count)], b_snd.at[n], b_rcv.at[n], on_z(0, True)
+        )
+
+    sib_send((0, 0), 0, 1)
     ring = {}
-
-    def ring_send(s):
-        ring[0, s] = send(
-            G.at[0, (1 - s) % NZ], G.at[0, (-s) % NZ], z_snd.at[0, s], z_rcv.at[0, s], on_z(1, False)
-        )
-        if s < 8:
-            ring[1, s] = send(
-                G.at[0, s - 1], G.at[0, s], z_snd.at[1, s], z_rcv.at[1, s], on_z(NZ - 1, False)
-            )
-
-    def sib_send(r):
-        ring["s", r] = send(G.at[0, r], G.at[1, r], b_snd.at[r], b_rcv.at[r], on_z(0, True))
-
     pumped = [0]
 
     def pump(upto):
-        while pumped[0] < min(upto, 8):
+        while pumped[0] < min(upto, 4):
             pumped[0] += 1
             s = pumped[0]
-            ring[0, s].wait_recv()
-            if s < 8:
-                ring[1, s].wait_recv()
-                ring_send(s + 1)
-            sib_send((-s) % NZ)
-            if s < 8:
-                sib_send(s)
-
-    ring_send(1)
-    sib_send(0)
+            up, down = (NZ - 2 * s, 2), (2 * s - 1, 1 if s == 4 else 2)
+            arrivals = first if s == 1 else [ring[0, s], ring[1, s]]
+            for copy in arrivals:
+                copy.wait_recv()
+            if s < 4:
+                n_down = 1 if s == 3 else 2
+                ring[0, s + 1] = send(
+                    G.at[0, pl.ds(up[0], 2)], G.at[0, pl.ds(up[0] - 2, 2)],
+                    z_snd.at[0, s], z_rcv.at[0, s], on_z(2, False),
+                )
+                ring[1, s + 1] = send(
+                    G.at[0, pl.ds(down[0], n_down)], G.at[0, pl.ds(down[0] + 2, n_down)],
+                    z_snd.at[1, s], z_rcv.at[1, s], on_z(NZ - 2, False),
+                )
+            sib_send((s, 0), *up)
+            sib_send((s, 1), *down)
+
+    got = set()
+
+    def need(step):
+        pump(step)
+        for key in sorted(sib):
+            if key[0] <= step and key not in got:
+                got.add(key)
+                sib[key].wait_recv()
 
     made = {}
 
@@ -235,9 +252,7 @@
 
     def partials(w):
         blocks = [(r, o) for r in WAVES[w] for o in (0, 1)]
-        pump(max(min(r, NZ - r) for r in WAVES[w]))
-        for r in WAVES[w]:
-            ring["s", r].wait_recv()
+        need(max((min(r, NZ - r) + 1) // 2 for r in WAVES[w]))
         tokens = jnp.concatenate([G[o, r, :, 0:256] for r, o in blocks], axis=0)
         grads = jnp.concatenate([G[o, r, :, 256:512] for r, o in blocks], axis=0)
         info_in = jnp.concatenate([G[o, r, :, 512:640] for r, o in blocks], axis=0)
@@ -362,7 +377,7 @@
                     gather_forward(w, h, 1)
 
     for tick in range(STAGES + LAG * (NW - 1)):
-        pump(2 + 2 * tick)
+        pump(1 + tick)
         for w in range(NW):
             k = tick - LAG * w
             if 0 <= k < STAGES:
@@ -371,11 +386,11 @@
     rows_x = X[...].reshape(512, 256)
     rows_g = GD[...].reshape(512, 256)
     stores = []
-    for t, (n_h, rhs, dst) in enumerate(((1, rows_x, gg), (2, rows_x, ug), (0, rows_g, dg))):
+    for t, (n_h, rhs) in enumerate(((1, rows_x), (2, rows_x), (0, rows_g))):
         for n in range(6):
             cols = H3[n_h, :, n * 256 : (n + 1) * 256]
             OUT[t, n * 256 : (n + 1) * 256, :] = dot_first(cols, rhs).astype(BF)
-        store = pltpu.make_async_copy(OUT.at[t], dst, o_sem.at[t])
+        store = pltpu.make_async_copy(OUT.at[t], grads_out.at[t], o_sem.at[t])
         store.start()
         stores.append(store)
 
@@ -400,7 +415,7 @@
     w_lo = (weights - w_hi.astype(F32)).astype(BF)
     e32 = expert_of(s32)
     by_k = jnp.concatenate(
-        [jnp.where(chosen & (e32 == ids[:, k : k + 1]), 1.0, 0.0) for k in range(8)], axis=0
+        [jnp.where(chosen & (e32.astype(F32) == ids_c[:, k : k + 1]), 1.0, 0.0) for k in range(8)], axis=0
     ).astype(BF)
     for copy in back.values():
         copy.wait_recv()
@@ -409,13 +424,13 @@
     back_rg = RR[:, :, :, 512:640].reshape(512, 128)
     lo_out[...] = (dot_plain(w_hi, back_eo) + dot_plain(w_lo, back_eo)).astype(BF)
     tg_out[...] = dot_plain(jnp.where(chosen, 1.0, 0.0).astype(BF), back_bo).astype(BF)
-    both = dot_plain(by_k, back_rg)
-    both = both + pltpu.roll(both, 64, 1)
-    k_i = lax.broadcasted_iota(jnp.int32, (32, 8), 1)
-    grad = jnp.zeros((32, 8), F32)
+    row = lax.broadcasted_iota(jnp.int32, (16, 128), 0)
+    col = lax.broadcasted_iota(jnp.int32, (16, 128), 1)
+    halves = jnp.where((col == row * 64) & (row < 2), 1.0, 0.0).astype(BF)
+    both = dot_last(dot_last(halves, back_rg).astype(BF), by_k)
+    both = both[0:1] + both[1:2]
     for k in range(8):
-        grad = grad + jnp.where(k_i == k, both[32 * k : 32 * k + 32, 0:1], 0.0)
-    rg_out[...] = grad
+        rg_out[k : k + 1, :] = both[:, 32 * k : 32 * k + 32]
 
     for store in stores:
         store.wait()
@@ -423,23 +438,38 @@
         copy.wait_send()
 
 
+def copy_out(lo, tg, rg, grads, lo_out, tg_out, rg_out, gg, ug, dg, LO, TG, RG, B, i_sem, o_sem):
+    pairs = [(lo, LO, lo_out), (tg, TG, tg_out), (rg, RG, rg_out)]
+    for t, dst in enumerate((gg, ug, dg)):
+        for n in (0, 1):
+            at = pl.ds(768 * n, 768)
+            pairs.append((grads.at[t, at], B.at[t, at], dst.at[at]))
+    ins = [pltpu.make_async_copy(a, b, i_sem.at[n]) for n, (a, b, _) in enumerate(pairs)]
+    outs = [pltpu.make_async_copy(b, c, o_sem.at[n]) for n, (_, b, c) in enumerate(pairs)]
+    for copy in ins:
+        copy.start()
+    for n in range(len(pairs)):
+        ins[n].wait()
+        outs[n].start()
+    for copy in outs:
+        copy.wait()
+
+
 def local(tokens, expert_ids, route_weights, gate_weight, up_weight, down_weight, output_grad):
     vmem = pl.BlockSpec(memory_space=pltpu.VMEM)
     hbm = pl.BlockSpec(memory_space=pl.ANY)
     wshape = jax.ShapeDtypeStruct((1536, 256), BF)
+    small = (
+        jax.ShapeDtypeStruct((32, 256), BF),
+        jax.ShapeDtypeStruct((32, 256), BF),
+        jax.ShapeDtypeStruct((8, 32), F32),
+    )
     dma = pltpu.SemaphoreType.DMA
-    lo, tg, rg, gg, ug, dg = pl.pallas_call(
+    results = pl.pallas_call(
         kernel,
-        out_shape=(
-            jax.ShapeDtypeStruct((32, 256), BF),
-            jax.ShapeDtypeStruct((32, 256), BF),
-            jax.ShapeDtypeStruct((32, 8), F32),
-            wshape,
-            wshape,
-            wshape,
-        ),
+        out_shape=small + (jax.ShapeDtypeStruct((3, 1536, 256), BF),),
         in_specs=[vmem, vmem, vmem, vmem, hbm, hbm, hbm],
-        out_specs=[vmem, vmem, vmem, hbm, hbm, hbm],
+        out_specs=[vmem, vmem, vmem, hbm],
         scratch_shapes=[
             pltpu.VMEM((3, 1536, 256), BF),
             pltpu.VMEM((2, NZ, 32, 640), BF),
@@ -462,10 +492,12 @@
             pltpu.VMEM((3, 1536, 256), BF),
             dma((3,)),
             dma((3,)),
-            dma((2, 9)),
-            dma((2, 9)),
-            dma((NZ,)),
-            dma((NZ,)),
+            dma((4,)),
+            dma((4,)),
+            dma((2, 4)),
+            dma((2, 4)),
+            dma((9,)),
+            dma((9,)),
             dma((NW, 2, 2, 2, 3)),
             dma((NW, 2, 2, 2, 3)),
             dma((NW, 2, 2, 2, 3)),
@@ -476,11 +508,27 @@
         compiler_params=pltpu.CompilerParams(
             collective_id=0, has_side_effects=True, vmem_limit_bytes=60 * 1024 * 1024
         ),
+        name="experts",
     )(
-        tokens, expert_ids, route_weights, output_grad,
+        tokens, expert_ids.T, route_weights.T, output_grad,
         gate_weight[0], up_weight[0], down_weight[0],
     )
-    return lo, tg, rg, gg[None], ug[None], dg[None]
+    lo, tg, rg, gg, ug, dg = pl.pallas_call(
+        copy_out,
+        out_shape=small + (wshape, wshape, wshape),
+        in_specs=[hbm] * 4,
+        out_specs=[hbm] * 6,
+        scratch_shapes=[
+            pltpu.VMEM((32, 256), BF),
+            pltpu.VMEM((32, 256), BF),
+            pltpu.VMEM((8, 32), F32),
+            pltpu.VMEM((3, 1536, 256), BF),
+            dma((9,)),
+            dma((9,)),
+        ],
+        name="copy_out",
+    )(*results)
+    return lo, tg, rg.T, gg[None], ug[None], dg[None]
 
 
 def solution(mesh):

time: 132 us -> 109 us (0.83)
  Pallas kernels: 122 us -> 108 us
  local copies, waits for them, and re-layouts: 9.17 us -> 0 us
    pallas_call x1 -> x2, Pallas kernels: 122 us -> 108 us  [the longest x1 106 us: local(): pl.pallas_call(kernel, out_shape=small + (jax.ShapeDtypeStruct((3, 1536,...]
    unnamed x22 -> x0, local copies, waits for them, and re-layouts: 9.17 us -> none
where the time goes in v2:
time: 109 us
  Pallas kernels  108 us (99%)
    pallas_call x1, Pallas kernels, local(): pl.pallas_call(kernel, out_shape=small + (jax.ShapeDtypeStruct((3, 1536,...  106 us
    pallas_call x1, Pallas kernels, local(): pl.pallas_call(copy_out, out_shape=small + (wshape, wshape, wshape), in_s...  2.59 us

profile of v2, /device:TPU:1, one launch (start us, length us, event | category | flops | bytes accessed | tf_op | source)
XLA Modules:
  0.0 109.0 jit_solution(5330506895453060214)
XLA Ops:
  0.6 105.8 %experts.1 = (bf16[32,256]{1,0:T(8,128)(2,1)}, bf16[32,256]{1,0:T(8,128)(2,1)}, f32[8,32]{1,0:T(8,128)}, bf16[3,1536,256]{2,1,0:T(8,128)(2,1)}) custom-call(bf16[32,256]{1,0:T(8,128)(2,1)} %tok.1, s32[8,32]{1,0:T(8,128)} %bitcast.12, f32[8,32]{1,0:T(8,128)} %bitcast.13, bf16[32,256]{1,0:T(8,128)(2,1)} %og.1, bf16[1536,256]{1,0:T(8,128)(2,1)} %bitcast.9, ...), custom_call_target="tpu_custom_call" | custom-call | tf_op jit(solution)/shard_map/experts/pallas_call | solution.py:468
  106.4 2.6 %copy_out.1 = (bf16[32,256]{1,0:T(8,128)(2,1)}, bf16[32,256]{1,0:T(8,128)(2,1)}, f32[8,32]{1,0:T(8,128)}, bf16[1536,256]{1,0:T(8,128)(2,1)}, bf16[1536,256]{1,0:T(8,128)(2,1)}, /*index=5*/bf16[1536,256]{1,0:T(8,128)(2,1)}) custom-call(bf16[32,256]{1,0:T(8,128)(2,1)} %get-tuple-element.16.lo, bf16[32,256]{1,0:T(8,128)(2,1)} %get-tuple-element.17.tg, ...), custom_call_target="tpu_custom_call" | custom-call | tf_op jit(solution)/shard_map/copy_out/pallas_call | solution.py:516

commit v3 on v2

--- a/solution.py
+++ b/solution.py
@@ -9,11 +9,18 @@
 BF = jnp.bfloat16
 F32 = jnp.float32
 
-WAVES = ((0, 15, 1, 14), (2, 13, 3, 12), (4, 11, 5, 10), (6, 9, 7, 8))
+WAVES = ((0, 15, 1, 14), (4, 11, 5, 10), (2, 13, 3, 12), (6, 9, 7, 8))
 NZ = 16
 NW = 4
-LAG = 1
-STAGES = 9
+ORDER = (
+    (0, 0), (1,), (2,), (1, 0, 1), (1, 0, 0), (0, 2), (2, 0, 1), (0, 1), (1, 2, 0), (1, 2, 1), (3,), (4,),
+    (1, 1, 1), (1, 1, 0), (0, 3), (2, 1, 0), (2, 2, 0), (2, 1, 1), (1, 3, 1), (1, 3, 0), (3, 1, 1), (2, 2, 1),
+    (3, 1, 0), (3, 2, 0), (2, 3, 1), (2, 3, 0), (2, 0, 0), (4, 1), (3, 2, 1), (3, 3, 1), (3, 3, 0), (5, 1, 1),
+    (3, 0, 1), (5, 1, 0), (4, 2), (3, 0, 0), (4, 3), (6, 1, 1), (6, 1, 0), (5, 3, 0), (5, 3, 1), (7, 1, 0),
+    (5, 2, 1), (7, 1, 1), (6, 3, 0), (6, 3, 1), (5, 2, 0), (4, 0), (8, 1), (7, 3, 0), (7, 3, 1), (5, 0, 0),
+    (6, 2, 1), (6, 2, 0), (5, 0, 1), (8, 3), (7, 2, 1), (6, 0, 1), (7, 2, 0), (6, 0, 0), (8, 2), (7, 0, 0),
+    (7, 0, 1), (8, 0),
+)
 
 
 def dot_last(a, b):
@@ -31,8 +38,8 @@
 def kernel(
     tok, ids, rw, og, wg, wu, wd,
     lo_out, tg_out, rg_out, grads_out,
-    W, G, X, GD, WC, S, M1P, M1M, RP, RM, Q1P, Q1M, QP, QM, A, H3, RET, RR, OUT,
-    w_sem, o_sem, n_snd, n_rcv, z_snd, z_rcv, b_snd, b_rcv, s_snd, s_rcv, a_snd, a_rcv, t_snd, t_rcv,
+    W, G, X, GD, WC, S, M1P, M1M, RP, RM, Q1P, Q1M, QP, QM, A, H3, RET, RR, RETG, RRG, OUT,
+    w_sem, o_sem, n_snd, n_rcv, z_snd, z_rcv, b_snd, b_rcv, s_snd, s_rcv, a_snd, a_rcv, t_snd, t_rcv, g_snd, g_rcv,
 ):
     dp = lax.axis_index("dp")
     e = lax.axis_index("expert")
@@ -105,7 +112,7 @@
         return copy
 
     first = []
-    for n, step in enumerate((1, NZ - 1, 2, NZ - 2)):
+    for n, step in enumerate((2, NZ - 2, 1, NZ - 1)):
         first.append(
             send(G.at[0, 0], G.at[0, NZ - step], n_snd.at[n], n_rcv.at[n], on_z(step, False))
         )
@@ -312,6 +319,7 @@
             gather_start(w, h, 0)
 
     lane16 = lax.broadcasted_iota(jnp.int32, (16, 128), 1)
+    row16 = lax.broadcasted_iota(jnp.int32, (16, 128), 0)
 
     def in_two(v):
         top = v.astype(BF).astype(F32)
@@ -340,48 +348,49 @@
         for j in range(8):
             r, o = WAVES[w][j // 2], j % 2
             v = A[w, 0, j // 2, 2 * o, 9].astype(F32) + A[w, 0, j // 2, 2 * o + 1, 9].astype(F32)
-            v = in_two(v + pltpu.roll(v, 64, 1))
+            v = v + pltpu.roll(v, 64, 1)
+            v = jnp.sum(jnp.where(row16 == lane16, v, 0.0), axis=0, keepdims=True)
             local = r == 0 and o == 0
             to = RR.at[0, 0] if local else RET.at[w, j]
             to[:, 0:256] = eo[16 * j : 16 * j + 16]
             to[:, 256:512] = bo[16 * j : 16 * j + 16]
-            to[:, 512:640] = v
+            (RRG.at[0, 0] if local else RETG.at[w, j])[...] = v
             if not local:
                 m = (NZ - r) % NZ
                 back[o, m] = send(
                     RET.at[w, j], RR.at[o, m], t_snd.at[o, m], t_rcv.at[o, m], on_z(r, o == 1)
                 )
-
-    def stage(k, w):
+                back["g", o, m] = send(
+                    RETG.at[w, j], RRG.at[o, m], g_snd.at[o, m], g_rcv.at[o, m], on_z(r, o == 1)
+                )
+
+    def stage(k, w, h=0):
         if k == 0:
             partials(w)
+        elif k == 1:
+            reduce_merge(w, h, 0)
+        elif k == 2:
+            reduce_end(w, h, 0)
+            reduce_start(w, h, 1)
+        elif k == 3:
+            reduce_merge(w, h, 1)
         elif k == 4:
             nonlinear(w)
-        elif k == 8:
+        elif k == 5:
+            gather_forward(w, h, 0)
+        elif k == 6:
+            gather_end(w, h, 0)
+            gather_start(w, h, 1)
+        elif k == 7:
+            gather_forward(w, h, 1)
+        else:
             results(w)
+
+    for item in ORDER:
+        if len(item) == 1:
+            pump(item[0])
         else:
-            for h in (0, 1):
-                if k == 1:
-                    reduce_merge(w, h, 0)
-                elif k == 2:
-                    reduce_end(w, h, 0)
-                    reduce_start(w, h, 1)
-                elif k == 3:
-                    reduce_merge(w, h, 1)
-                elif k == 5:
-                    gather_forward(w, h, 0)
-                elif k == 6:
-                    gather_end(w, h, 0)
-                    gather_start(w, h, 1)
-                elif k == 7:
-                    gather_forward(w, h, 1)
-
-    for tick in range(STAGES + LAG * (NW - 1)):
-        pump(1 + tick)
-        for w in range(NW):
-            k = tick - LAG * w
-            if 0 <= k < STAGES:
-                stage(k, w)
+            stage(*item)
 
     rows_x = X[...].reshape(512, 256)
     rows_g = GD[...].reshape(512, 256)
@@ -421,13 +430,19 @@
         copy.wait_recv()
     back_eo = RR[:, :, :, 0:256].reshape(512, 256)
     back_bo = RR[:, :, :, 256:512].reshape(512, 256)
-    back_rg = RR[:, :, :, 512:640].reshape(512, 128)
     lo_out[...] = (dot_plain(w_hi, back_eo) + dot_plain(w_lo, back_eo)).astype(BF)
     tg_out[...] = dot_plain(jnp.where(chosen, 1.0, 0.0).astype(BF), back_bo).astype(BF)
-    row = lax.broadcasted_iota(jnp.int32, (16, 128), 0)
-    col = lax.broadcasted_iota(jnp.int32, (16, 128), 1)
-    halves = jnp.where((col == row * 64) & (row < 2), 1.0, 0.0).astype(BF)
-    both = dot_last(dot_last(halves, back_rg).astype(BF), by_k)
+    rg_b = RRG[...].reshape(32, 128)
+    rg_hi = rg_b.astype(BF)
+    rg_lo = (rg_b - rg_hi.astype(F32)).astype(BF)
+    spread = jnp.where(l_i == s_i % 16, 1.0, 0.0).astype(BF)
+    block = lax.broadcasted_iota(jnp.int32, (32, 512), 0) == s32 // 16
+    rows2 = [
+        jnp.sum(jnp.where(block, dot_plain(v, spread), 0.0), axis=0, keepdims=True)
+        for v in (rg_hi, rg_lo)
+    ]
+    first_row = lax.broadcasted_iota(jnp.int32, (16, 512), 0) == 0
+    both = dot_last(jnp.where(first_row, rows2[0], rows2[1]).astype(BF), by_k)
     both = both[0:1] + both[1:2]
     for k in range(8):
         rg_out[k : k + 1, :] = both[:, 32 * k : 32 * k + 32]
@@ -487,8 +502,10 @@
             pltpu.VMEM((NW, 2, 9, 16, 128), BF),
             pltpu.VMEM((NW, 2, 4, 4, 10, 16, 128), BF),
             pltpu.VMEM((3, 512, 1536), BF),
-            pltpu.VMEM((NW, 8, 16, 640), BF),
-            pltpu.VMEM((2, NZ, 16, 640), BF),
+            pltpu.VMEM((NW, 8, 16, 512), BF),
+            pltpu.VMEM((2, NZ, 16, 512), BF),
+            pltpu.VMEM((NW, 8, 1, 128), F32),
+            pltpu.VMEM((2, NZ, 1, 128), F32),
             pltpu.VMEM((3, 1536, 256), BF),
             dma((3,)),
             dma((3,)),
@@ -502,6 +519,8 @@
             dma((NW, 2, 2, 2, 3)),
             dma((NW, 2, 2, 2, 3)),
             dma((NW, 2, 2, 2, 3)),
+            dma((2, NZ)),
+            dma((2, NZ)),
             dma((2, NZ)),
             dma((2, NZ)),
         ],

time: 109 us -> 102 us (0.936)
  Pallas kernels: 108 us -> 101 us
    pallas_call x1, Pallas kernels: 106 us -> 98.1 us  [local(): pl.pallas_call(kernel, out_shape=small + (jax.ShapeDtypeStruct((3, 1536,...]
where the time goes in v3:
time: 102 us; the launch traced here: 101 us
  Pallas kernels  101 us (99%)
    pallas_call x1, Pallas kernels, local(): pl.pallas_call(kernel, out_shape=small + (jax.ShapeDtypeStruct((3, 1536,...  98.1 us
    pallas_call x1, Pallas kernels, local(): pl.pallas_call(copy_out, out_shape=small + (wshape, wshape, wshape), in_s...  2.59 us

profile of v3, /device:TPU:1, one launch (start us, length us, event | category | flops | bytes accessed | tf_op | source)
XLA Modules:
  0.0 101.3 jit_solution(6453853068717566581)
XLA Ops:
  0.6 98.1 %experts.1 = (bf16[32,256]{1,0:T(8,128)(2,1)}, bf16[32,256]{1,0:T(8,128)(2,1)}, f32[8,32]{1,0:T(8,128)}, bf16[3,1536,256]{2,1,0:T(8,128)(2,1)}) custom-call(bf16[32,256]{1,0:T(8,128)(2,1)} %tok.1, s32[8,32]{1,0:T(8,128)} %bitcast.12, f32[8,32]{1,0:T(8,128)} %bitcast.13, bf16[32,256]{1,0:T(8,128)(2,1)} %og.1, bf16[1536,256]{1,0:T(8,128)(2,1)} %bitcast.9, ...), custom_call_target="tpu_custom_call" | custom-call | tf_op jit(solution)/shard_map/experts/pallas_call | solution.py:483
  98.7 2.6 %copy_out.1 = (bf16[32,256]{1,0:T(8,128)(2,1)}, bf16[32,256]{1,0:T(8,128)(2,1)}, f32[8,32]{1,0:T(8,128)}, bf16[1536,256]{1,0:T(8,128)(2,1)}, bf16[1536,256]{1,0:T(8,128)(2,1)}, /*index=5*/bf16[1536,256]{1,0:T(8,128)(2,1)}) custom-call(bf16[32,256]{1,0:T(8,128)(2,1)} %get-tuple-element.16.lo, bf16[32,256]{1,0:T(8,128)(2,1)} %get-tuple-element.17.tg, ...), custom_call_target="tpu_custom_call" | custom-call | tf_op jit(solution)/shard_map/copy_out/pallas_call | solution.py:535

commit v4 on v3

--- a/solution.py
+++ b/solution.py
@@ -13,13 +13,13 @@
 NZ = 16
 NW = 4
 ORDER = (
-    (0, 0), (1,), (2,), (1, 0, 1), (1, 0, 0), (0, 2), (2, 0, 1), (0, 1), (1, 2, 0), (1, 2, 1), (3,), (4,),
-    (1, 1, 1), (1, 1, 0), (0, 3), (2, 1, 0), (2, 2, 0), (2, 1, 1), (1, 3, 1), (1, 3, 0), (3, 1, 1), (2, 2, 1),
-    (3, 1, 0), (3, 2, 0), (2, 3, 1), (2, 3, 0), (2, 0, 0), (4, 1), (3, 2, 1), (3, 3, 1), (3, 3, 0), (5, 1, 1),
-    (3, 0, 1), (5, 1, 0), (4, 2), (3, 0, 0), (4, 3), (6, 1, 1), (6, 1, 0), (5, 3, 0), (5, 3, 1), (7, 1, 0),
-    (5, 2, 1), (7, 1, 1), (6, 3, 0), (6, 3, 1), (5, 2, 0), (4, 0), (8, 1), (7, 3, 0), (7, 3, 1), (5, 0, 0),
-    (6, 2, 1), (6, 2, 0), (5, 0, 1), (8, 3), (7, 2, 1), (6, 0, 1), (7, 2, 0), (6, 0, 0), (8, 2), (7, 0, 0),
-    (7, 0, 1), (8, 0),
+    (1,), (0, 0), (2,), (1, 0, 1), (1, 0, 0), (0, 2), (2, 0, 1), (0, 1), (1, 2, 1), (3, 0, 1), (3,), (4,),
+    (1, 2, 0), (1, 1, 1), (1, 1, 0), (0, 3), (2, 1, 0), (2, 1, 1), (2, 2, 1), (2, 2, 0), (1, 3, 1), (1, 3, 0),
+    (3, 1, 1), (3, 1, 0), (3, 2, 0), (2, 3, 1), (2, 3, 0), (4, 1, 1), (4, 1, 0), (3, 2, 1), (3, 3, 1),
+    (3, 3, 0), (5, 1, 0), (5, 1, 1), (2, 0, 0), (4, 2, 1), (4, 2, 0), (4, 3, 1), (4, 3, 0), (6, 1, 0),
+    (6, 1, 1), (5, 3, 1), (3, 0, 0), (5, 3, 0), (7, 1, 0), (7, 1, 1), (5, 2, 0), (4, 0, 1), (5, 2, 1),
+    (6, 3, 1), (6, 3, 0), (4, 0, 0), (8, 1), (7, 3, 0), (7, 3, 1), (6, 2, 0), (5, 0, 1), (6, 2, 1), (8, 3),
+    (7, 2, 0), (5, 0, 0), (7, 2, 1), (6, 0, 1), (6, 0, 0), (8, 2), (7, 0, 0), (7, 0, 1), (8, 0),
 )
 
 
@@ -297,26 +297,28 @@
         for h in (0, 1):
             reduce_start(w, h, 0)
 
-    def nonlinear(w):
-        rg = jnp.zeros((16, 1), F32)
-        for h in (0, 1):
-            total = reduce_end(w, h, 1)
-            i, j = pos[h], pos[1 - h]
-            for k in range(3):
-                gate, up, hid = total[3 * k], total[3 * k + 1], total[3 * k + 2]
-                sig = jax.nn.sigmoid(gate)
-                silu = gate * sig
-                act = (silu * up).astype(BF)
-                A[w, h, i, j, 3 * k] = act
-                A[w, h, i, j, 3 * k + 1] = (hid * up * (sig * (1.0 + gate * (1.0 - sig)))).astype(BF)
-                A[w, h, i, j, 3 * k + 2] = (hid * silu).astype(BF)
-                rg = rg + jnp.sum(act.astype(F32) * hid, axis=1, keepdims=True)
-        wc = WC[w, 2 * x + y // 2]
-        used = wc > 0.0
-        rg = jnp.where(used, rg / jnp.where(used, wc, 1.0), 0.0)
-        A[w, 0, x, y, 9] = in_two(rg)
-        for h in (0, 1):
-            gather_start(w, h, 0)
+    route = {}
+
+    def nonlinear(w, h):
+        rg = route.get(w, jnp.zeros((16, 1), F32))
+        total = reduce_end(w, h, 1)
+        i, j = pos[h], pos[1 - h]
+        for k in range(3):
+            gate, up, hid = total[3 * k], total[3 * k + 1], total[3 * k + 2]
+            sig = jax.nn.sigmoid(gate)
+            silu = gate * sig
+            act = (silu * up).astype(BF)
+            A[w, h, i, j, 3 * k] = act
+            A[w, h, i, j, 3 * k + 1] = (hid * up * (sig * (1.0 + gate * (1.0 - sig)))).astype(BF)
+            A[w, h, i, j, 3 * k + 2] = (hid * silu).astype(BF)
+            rg = rg + jnp.sum(act.astype(F32) * hid, axis=1, keepdims=True)
+        route[w] = rg
+        if h == 0:
+            wc = WC[w, 2 * x + y // 2]
+            used = wc > 0.0
+            rg = jnp.where(used, rg / jnp.where(used, wc, 1.0), 0.0)
+            A[w, 0, x, y, 9] = in_two(rg)
+        gather_start(w, h, 0)
 
     lane16 = lax.broadcasted_iota(jnp.int32, (16, 128), 1)
     row16 = lax.broadcasted_iota(jnp.int32, (16, 128), 0)
@@ -375,7 +377,7 @@
         elif k == 3:
             reduce_merge(w, h, 1)
         elif k == 4:
-            nonlinear(w)
+            nonlinear(w, h)
         elif k == 5:
             gather_forward(w, h, 0)
         elif k == 6:
@@ -426,6 +428,8 @@
     by_k = jnp.concatenate(
         [jnp.where(chosen & (e32.astype(F32) == ids_c[:, k : k + 1]), 1.0, 0.0) for k in range(8)], axis=0
     ).astype(BF)
+    for copy in sent:
+        copy.wait_send()
     for copy in back.values():
         copy.wait_recv()
     back_eo = RR[:, :, :, 0:256].reshape(512, 256)
@@ -449,8 +453,6 @@
 
     for store in stores:
         store.wait()
-    for copy in sent:
-        copy.wait_send()
 
 
 def copy_out(lo, tg, rg, grads, lo_out, tg_out, rg_out, gg, ug, dg, LO, TG, RG, B, i_sem, o_sem):

time: 102 us -> 101 us (level)
  Pallas kernels: 101 us -> 99.8 us
where the time goes in v4:
time: 101 us; the launch traced here: 100 us
  Pallas kernels  99.8 us (99%)
    pallas_call x1, Pallas kernels, local(): pl.pallas_call(kernel, out_shape=small + (jax.ShapeDtypeStruct((3, 1536,...  97.2 us
    pallas_call x1, Pallas kernels, local(): pl.pallas_call(copy_out, out_shape=small + (wshape, wshape, wshape), in_s...  2.59 us

profile of v4, /device:TPU:1, one launch (start us, length us, event | category | flops | bytes accessed | tf_op | source)
XLA Modules:
  0.0 100.4 jit_solution(968589205431241771)
XLA Ops:
  0.6 97.2 %experts.1 = (bf16[32,256]{1,0:T(8,128)(2,1)}, bf16[32,256]{1,0:T(8,128)(2,1)}, f32[8,32]{1,0:T(8,128)}, bf16[3,1536,256]{2,1,0:T(8,128)(2,1)}) custom-call(bf16[32,256]{1,0:T(8,128)(2,1)} %tok.1, s32[8,32]{1,0:T(8,128)} %bitcast.12, f32[8,32]{1,0:T(8,128)} %bitcast.13, bf16[32,256]{1,0:T(8,128)(2,1)} %og.1, bf16[1536,256]{1,0:T(8,128)(2,1)} %bitcast.9, ...), custom_call_target="tpu_custom_call" | custom-call | tf_op jit(solution)/shard_map/experts/pallas_call | solution.py:485
  97.9 2.6 %copy_out.1 = (bf16[32,256]{1,0:T(8,128)(2,1)}, bf16[32,256]{1,0:T(8,128)(2,1)}, f32[8,32]{1,0:T(8,128)}, bf16[1536,256]{1,0:T(8,128)(2,1)}, bf16[1536,256]{1,0:T(8,128)(2,1)}, /*index=5*/bf16[1536,256]{1,0:T(8,128)(2,1)}) custom-call(bf16[32,256]{1,0:T(8,128)(2,1)} %get-tuple-element.16.lo, bf16[32,256]{1,0:T(8,128)(2,1)} %get-tuple-element.17.tg, ...), custom_call_target="tpu_custom_call" | custom-call | tf_op jit(solution)/shard_map/copy_out/pallas_call | solution.py:537
